TPU v7x, 32 devices: a whole 2x2x4 slice. The times are simulated.
32 devices in a mesh: tmpl: 2 (over y), freq: 16 (over z, x, core).
Axes of the slice: x: 2, y: 2, z: 4, core: 2. Of those that a mesh axis runs over, the one named last changes fastest.
Arguments:
- strain: bfloat16 [3, 1024, 512], P(None, 'freq'), may hold values from -6 to 6
- gate_start: int32 [3, 2], replicated, may hold values from 0 to 520191
- psd_inverse: float32 [3, 512, 1024], P(None, 'freq'), may hold values from 0.5 to 6, as said below
- templates: bfloat16 [8, 2, 512, 1024], P('tmpl', None, 'freq'), may hold values from -6 to 6
- basis: bfloat16 [3, 4, 512, 1024], P(None, None, 'freq'), may hold values from -2.5 to 4.5
Outputs:
- best: float32 [512, 1024], P('tmpl', 'freq')
Inputs may be any that keep to these rules, and one draw needn't show every extreme that they name: `psd_inverse`: positive weights.
All inputs are finite; a program needn't handle non-finite values.
Results may differ from a plain program's by a relative error of at most 0.004.
Values may be sent and summed in bfloat16 or wider, within the bound.
No kernel may reach another device: no remote copies, remote signals or barrier semaphores. Data moves between devices by JAX's collectives and lax.ppermute only.
A program may use at most 128 MiB of HBM per device.

v0:
```python
import math
import jax
import jax.numpy as jnp
from jax import lax
from jax.sharding import PartitionSpec as P

N1 = 512
N2 = 1024
DET = 3
RESP = 5
GATE_LEN = 4096


def fourier_table(length, orient):
    indices = jnp.arange(length, dtype=jnp.int32)
    products = indices[:, None] * indices[None, :] % length
    angles = products.astype(jnp.float32) * (2.0 * math.pi / length)
    return (jnp.cos(angles), orient * jnp.sin(angles))


def real_table(length):
    cosines, sine_part = fourier_table(length, -1.0)
    return jnp.concatenate([cosines, sine_part], axis=1).astype(jnp.bfloat16)


def complex_table(length, orient):
    cosines, sine_part = fourier_table(length, orient)
    upper_row = jnp.concatenate([cosines, sine_part], axis=1)
    bottom = jnp.concatenate([-sine_part, cosines], axis=1)
    return jnp.stack([upper_row, bottom], axis=0).astype(jnp.bfloat16)


def twiddle_table(row_index, col_index, modulus, orient):
    products = row_index[:, None] * col_index[None, :] % modulus
    angles = products.astype(jnp.float32) * (2.0 * math.pi / modulus)
    return (jnp.cos(angles), orient * jnp.sin(angles))


def rotate(real_part, imag_part, cosines, sine_part):
    return (
        real_part * cosines - imag_part * sine_part,
        real_part * sine_part + imag_part * cosines,
    )


def statistic(real_lags, imag_lags, variance, projection, spread):
    base_real = real_lags[:, 0]
    base_imag = imag_lags[:, 0]
    head_term = (base_real * base_real + base_imag * base_imag) / (
        N1 * N2 * variance[:, None, None]
    )
    remain_real = real_lags[:, 1:] - projection[:, :, None, None] * base_real[:, None]
    remain_imag = imag_lags[:, 1:] - projection[:, :, None, None] * base_imag[:, None]
    tail_term = jnp.sum(
        (remain_real * remain_real + remain_imag * remain_imag) / spread[:, :, None, None], axis=1
    )
    return jnp.sum(head_term + tail_term, axis=0) / (DET * RESP)


def on_device(strain, gate_start, psd_inverse, templates, basis):
    freq_place = lax.axis_index("freq")
    local_cols = strain.shape[1]
    local_rows = psd_inverse.shape[1]
    modulus = N1 * N2
    col_global = freq_place * local_cols + jnp.arange(local_cols, dtype=jnp.int32)
    sample = N2 * jnp.arange(N1, dtype=jnp.int32)[None, :] + col_global[:, None]
    starts = gate_start[:, :, None, None]
    inside = (sample[None, None] >= starts) & (sample[None, None] < starts + GATE_LEN)
    keep_mask = jnp.where(jnp.any(inside, axis=1), 0.0, 1.0).astype(strain.dtype)
    gated_strain = strain * keep_mask
    section = jnp.einsum(
        "dcn,nq->dqc", gated_strain, real_table(N1), preferred_element_type=jnp.float32
    )
    section = section.reshape(DET, 2, N1, local_cols)
    cosines, sine_part = twiddle_table(jnp.arange(N1, dtype=jnp.int32), col_global, modulus, -1.0)
    real_part, imag_part = rotate(section[:, 0], section[:, 1], cosines, sine_part)
    section_one = jnp.stack([real_part, imag_part], axis=1).astype(jnp.bfloat16)
    spectra = lax.all_to_all(section_one, "freq", split_axis=2, concat_axis=3, tiled=True)
    spectrum = jnp.einsum(
        "dpkc,pcq->dkq", spectra, complex_table(N2, -1.0), preferred_element_type=jnp.float32
    )
    data_real = spectrum[..., :N2] * psd_inverse
    data_imag = spectrum[..., N2:] * psd_inverse
    basis_float = basis.astype(jnp.float32)
    responses = jnp.concatenate(
        [jnp.ones((DET, 1, local_rows, N2), jnp.float32), basis_float], axis=1
    )
    template_real = templates[:, 0].astype(jnp.float32)
    template_imag = templates[:, 1].astype(jnp.float32)
    template_count = templates.shape[0]
    product_real = (
        data_real[None] * template_real[:, None] + data_imag[None] * template_imag[:, None]
    )
    product_imag = (
        data_imag[None] * template_real[:, None] - data_real[None] * template_imag[:, None]
    )
    filtered = jnp.stack(
        [product_real[:, :, None] * responses[None], product_imag[:, :, None] * responses[None]],
        axis=3,
    )
    filtered = filtered.astype(jnp.bfloat16).reshape(-1, 2, local_rows, N2)
    lag_section = jnp.einsum(
        "ipkm,pmq->ikq", filtered, complex_table(N2, 1.0), preferred_element_type=jnp.float32
    )
    row_global = freq_place * local_rows + jnp.arange(local_rows, dtype=jnp.int32)
    back_cos, back_sin = twiddle_table(row_global, jnp.arange(N2, dtype=jnp.int32), modulus, 1.0)
    real_part, imag_part = rotate(lag_section[..., :N2], lag_section[..., N2:], back_cos, back_sin)
    lag_one = jnp.stack([real_part, imag_part], axis=1).astype(jnp.bfloat16)
    table_row = complex_table(N1, 1.0)
    lags = jnp.einsum(
        "ipkc,pkq->iqc",
        lax.all_to_all(lag_one, "freq", split_axis=3, concat_axis=2, tiled=True),
        table_row,
        preferred_element_type=jnp.float32,
    )
    weight = (psd_inverse * psd_inverse)[None] * (
        template_real * template_real + template_imag * template_imag
    )[:, None]
    variance_local = jnp.sum(weight, axis=(2, 3))
    intersection_local = jnp.einsum("tdkm,djkm->tdj", weight, basis_float)
    variance, intersection = lax.psum((variance_local, intersection_local), "freq")
    projection = intersection / variance[..., None]
    centred = basis_float[None] - projection[..., None, None]
    spread_local = jnp.sum(weight[:, :, None] * centred * centred, axis=(3, 4))
    spread = modulus * lax.psum(spread_local, "freq")
    batched = jax.vmap(statistic)
    lag_grid = lags.reshape(template_count, DET, RESP, 2, N1, local_cols)
    statistics = batched(lag_grid[:, :, :, 0], lag_grid[:, :, :, 1], variance, projection, spread)
    best_local = jnp.max(statistics, axis=0)
    received = lax.all_to_all(best_local[None], "tmpl", split_axis=1, concat_axis=0, tiled=True)
    return jnp.max(received, axis=0)


def solution(mesh):
    placed = (
        P(None, "freq", None),
        P(),
        P(None, "freq", None),
        P("tmpl", None, "freq", None),
        P(None, None, "freq", None),
    )
    return jax.shard_map(
        on_device, mesh=mesh, in_specs=placed, out_specs=P("tmpl", "freq"), check_vma=False
    )
```

profile of v0, /device:TPU:0, one launch (start us, length us, event | category | flops | bytes accessed | tf_op | source)
XLA Modules:
  0.0 587.6 jit_solution(1520136712507840119)
XLA Ops:
  0.0 4.3 multiply_convert_fusion.3
  4.4 0.7 broadcast_add_fusion.1
  5.1 0.8 copy.89
  5.9 1.1 fusion.70
  7.4 1.3 convolution_bitcast_fusion.1
  10.0 0.9 copy.115
  10.8 0.9 copy.116
  11.7 1.7 subtract_convert_fusion.1
  13.4 2.1 fusion.82
  15.5 1.3 reshape.229
  16.8 8.0 %all-to-all-start = ((bf16[16,2,6144]{2,1,0:T(2,128)(2,1)}), bf16[16,2,6144]{2,1,0:T(2,128)(2,1)}, u32[]{:S(2)}, u32[]{:S(2)}) async-start(bf16[16,2,6144]{2,1,0:T(2,128)(2,1)} %reshape.229), calls=%async_computation | async-start | bytes 786432 | tf_op jit(solution)/shard_map/all_to_all | solution.py:78
  24.8 16.6 %negate_convert_fusion = (bf16[1024,1024]{1,0:T(8,128)(2,1)S(1)}, bf16[1024,1024]{1,0:T(8,128)(2,1)}) fusion(), kind=kLoop, calls=%fused_computation.41 | loop fusion | flops 19922944 | bytes 4194304 | tf_op jit(solution)/shard_map/convert.7
  41.5 17.8 %cosine_convert_fusion = (bf16[1024,1024]{1,0:T(8,128)(2,1)}, bf16[1024,1024]{1,0:T(8,128)(2,1)}) fusion(), kind=kLoop, calls=%fused_computation.43 | loop fusion | flops 17825792 | bytes 4194304 | tf_op jit(solution)/shard_map/convert.22
  59.3 16.4 %fusion.32 = bf16[1024,1024]{1,0:T(8,128)(2,1)} fusion(), kind=kLoop, calls=%fused_computation.55 | loop fusion | flops 15728640 | bytes 2097152 | tf_op jit(solution)/shard_map/convert.11
  75.6 1.0 convert_bitcast_fusion.1
  76.6 1.3 fusion.73
  77.9 1.5 concatenate.38
  79.4 9.4 %fusion.18 = (bf16[1,1024,2048]{2,1,0:T(8,128)(2,1)}, bf16[1,1024,2048]{2,1,0:T(8,128)(2,1)}, bf16[1,1024,2048]{2,1,0:T(8,128)(2,1)}, bf16[1,1024,2048]{2,1,0:T(8,128)(2,1)}) fusion(bf16[1024,1024]{1,0:T(8,128)(2,1)} %get-tuple-element.38, bf16[1024,1024]{1,0:T(8,128)(2,1)} %get-tuple-element.39, bf16[1024,1024]{1,0:T(8,128)(2,1)S(1)} %get-tuple-element.36, ...), kind=kLoop, calls=%fused_computation.36 | loop fusion | flops 29360128 | bytes 27262976 | tf_op jit(solution)/shard_map/stack | solution.py:30
  88.9 2.5 reshape.230
  92.4 4.4 fusion.28
  96.8 0.9 slice_multiply_fusion.1
  98.5 5.6 multiply_convert_fusion.1
  104.1 18.9 %fusion.13 = f32[60,32,2048]{2,1,0:T(8,128)S(1)} fusion(bf16[1,1024,2048]{2,1,0:T(8,128)(2,1)S(1)} %copy-done.2, bf16[1,1024,2048]{2,1,0:T(8,128)(2,1)S(1)} %copy-done.3, bf16[60,1,32,1024]{3,2,1,0:T(8,128)(2,1)} %bitcast.107, bf16[60,1,32,1024]{3,2,1,0:T(8,128)(2,1)} %bitcast.106), kind=kOutput, calls=%fused_computation.29 | convolution fusion | flops 16114253824 | bytes 31981568 | tf_op jit(solution)/shard_map/ipkm,pmq->ikq/dot_general | solution.py:102
  123.0 2.7 fusion.26
  125.7 3.7 pad_maximum_fusion
  129.4 28.5 %copy.95 = bf16[60,2,32,1024]{0,2,1,3:T(8,128)(2,1)} copy(bf16[60,2,32,1024]{3,2,0,1:T(8,128)(2,1)} %pad_maximum_fusion) | data formatting | bytes 15728640 | tf_op jit(solution)/shard_map/stack | solution.py:108
  157.9 46.8 %reshape.231 = bf16[16,2,122880]{2,1,0:T(2,128)(2,1)} reshape(bf16[1024,2,32,60]{3,2,1,0:T(8,128)(2,1)} %bitcast.97) | data formatting | bytes 15728640
  204.6 6.3 %all-to-all-start.1 = ((bf16[16,2,122880]{2,1,0:T(2,128)(2,1)}), bf16[16,2,122880]{2,1,0:T(2,128)(2,1)}, u32[]{:S(2)}, u32[]{:S(2)}) async-start(bf16[16,2,122880]{2,1,0:T(2,128)(2,1)} %reshape.231), calls=%async_computation.1 | async-start | bytes 15728640 | tf_op jit(solution)/shard_map/all_to_all | solution.py:112
  211.6 4.0 negate_convert_fusion.2
  215.6 1.6 fusion.38
  217.2 1.5 fusion.35
  218.7 0.8 broadcast_multiply_fusion
  219.6 154.7 %all-reduce.1 = (f32[4,3,4]{2,0,1:T(4,128)S(1)}, f32[4,3]{0,1:T(4,128)S(1)}) all-reduce(f32[4,3,4]{2,0,1:T(4,128)S(1)} %fusion.35, f32[4,3]{0,1:T(4,128)S(1)} %get-tuple-element.24), channel_id=1, replica_groups=mesh['tmpl'=2,'freq'=16] {'freq'}, use_global_device_ids=true, to_apply=%region_3.4 | all-reduce | flops 60 | bytes 480 | tf_op jit(solution)/shard_map/psum | solution.py:121
  374.5 0.9 copy.104
  375.4 1.0 fusion.7
  376.4 51.9 %psum.23 = f32[4,3,4]{2,0,1:T(4,128)S(1)} all-reduce(f32[4,3,4]{2,0,1:T(4,128)S(1)} %copy.106), channel_id=1, replica_groups=mesh['tmpl'=2,'freq'=16] {'freq'}, use_global_device_ids=true, to_apply=%region_5.6 | all-reduce | flops 48 | bytes 384 | tf_op jit(solution)/shard_map/psum | solution.py:125
  428.6 53.3 %reshape.232 = bf16[1024,2,32,60]{3,2,1,0:T(8,128)(2,1)} reshape(bf16[16,2,122880]{2,1,0:T(2,128)(2,1)} %all-to-all-done.1) | data formatting | bytes 15728640
  481.9 31.2 %copy.96 = bf16[60,2,32,16,64]{4,2,3,1,0:T(8,128)(2,1)} copy(bf16[60,2,32,16,64]{0,2,1,4,3:T(8,128)(2,1)} %bitcast.98) | data formatting | bytes 15728640 | tf_op jit(solution)/shard_map/all_to_all | solution.py:112
  513.1 15.0 %convolution_bitcast_fusion = f32[60,1024,64]{1,2,0:T(8,128)} fusion(bf16[60,2,512,64]{3,2,1,0:T(8,128)(2,1)} %bitcast.105, bf16[1,512,1024]{2,1,0:T(8,128)(2,1)S(1)} %copy-done.12, bf16[1,512,1024]{2,1,0:T(8,128)(2,1)S(1)} %copy-done.11), kind=kOutput, calls=%fused_computation.1 | convolution fusion | flops 8057257984 | bytes 25690112 | tf_op jit(solution)/shard_map/ipkc,pkq->iqc/dot_general | solution.py:110
  528.0 20.8 %reshape.220 = f32[4,3,5,2,512,64]{4,3,5,2,1,0:T(2,128)} reshape(f32[60,1024,64]{1,2,0:T(8,128)} %convolution_bitcast_fusion) | data formatting | bytes 31457280 | tf_op jit(solution)/shard_map/reshape | solution.py:127
  548.9 17.2 %fusion.80 = (f32[4,3,5,1,512,64]{4,3,5,2,1,0:T(1,128)S(1)}, f32[4,3,5,1,512,64]{4,3,5,2,1,0:T(1,128)}) fusion(f32[4,3,5,2,512,64]{4,3,5,2,1,0:T(2,128)} %reshape.220), kind=kLoop, calls=%fused_computation.143 | loop fusion | bytes 31457280 | tf_op jit(solution)/shard_map/slice | solution.py:128
  566.1 4.3 copy.123
  570.6 1.6 copy.124
  572.4 2.7 fusion.12
  576.5 1.3 reduce.2
  578.0 7.1 %all_to_all.48 = f32[2,1,16384]{2,1,0:T(1,128)S(1)} all-to-all(f32[2,1,16384]{2,1,0:T(1,128)S(1)} %reshape.233), channel_id=1, replica_groups=mesh['tmpl'=2,'freq'=16] {'tmpl'}, dimensions={0} | all-to-all | bytes 262144 | tf_op jit(solution)/shard_map/all_to_all | solution.py:130
  585.0 1.0 reduce.3
  586.4 0.7 copy.109
  (64 shorter events, 6.7 us)
Async XLA Ops:
  4.4 3.0 copy-start.8
  16.8 72.0 %all-to-all-start = ((bf16[16,2,6144]{2,1,0:T(2,128)(2,1)}), bf16[16,2,6144]{2,1,0:T(2,128)(2,1)}, u32[]{:S(2)}, u32[]{:S(2)}) async-start(bf16[16,2,6144]{2,1,0:T(2,128)(2,1)} %reshape.229), calls=%async_computation | async-start | bytes 786432 | tf_op jit(solution)/shard_map/all_to_all | solution.py:78
  24.8 50.8 %copy-start.6 = (bf16[4,2,32,1024]{3,2,1,0:T(8,128)(2,1)S(1)}, bf16[4,2,32,1024]{3,2,1,0:T(8,128)(2,1)}, u32[]{:S(2)}) copy-start(bf16[4,2,32,1024]{3,2,1,0:T(8,128)(2,1)} %param.8) | copy-start | bytes 1572868
  41.5 36.4 %copy-start.4 = (bf16[3,4,32,1024]{3,2,1,0:T(8,128)(2,1)S(1)}, bf16[3,4,32,1024]{3,2,1,0:T(8,128)(2,1)}, u32[]{:S(2)}) copy-start(bf16[3,4,32,1024]{3,2,1,0:T(8,128)(2,1)} %param.9) | copy-start | bytes 2359300
  76.6 2.8 copy-start
  92.4 4.4 copy-start.14
  92.4 5.3 copy-start.5
  96.8 1.7 copy-start.1
  98.5 5.6 copy-start.2
  98.5 5.6 copy-start.3
  104.1 18.9 %copy-start.13 = (f32[32,1024]{1,0:T(8,128)S(1)}, f32[32,1024]{1,0:T(8,128)}, u32[]{:S(2)}) copy-start(f32[32,1024]{1,0:T(8,128)} %get-tuple-element.33) | copy-start | bytes 393220
  204.6 6.5 %copy-start.7 = (bf16[4,2,32,1024]{3,2,1,0:T(8,128)(2,1)S(1)}, bf16[4,2,32,1024]{3,2,1,0:T(8,128)(2,1)}, u32[]{:S(2)}) copy-start(bf16[4,2,32,1024]{3,2,1,0:T(8,128)(2,1)} %param.8) | copy-start | bytes 1572868
  204.6 224.0 %all-to-all-start.1 = ((bf16[16,2,122880]{2,1,0:T(2,128)(2,1)}), bf16[16,2,122880]{2,1,0:T(2,128)(2,1)}, u32[]{:S(2)}, u32[]{:S(2)}) async-start(bf16[16,2,122880]{2,1,0:T(2,128)(2,1)} %reshape.231), calls=%async_computation.1 | async-start | bytes 15728640 | tf_op jit(solution)/shard_map/all_to_all | solution.py:112
  210.9 4.7 copy-start.9
  210.9 6.3 %copy-start.10 = (f32[3,32,1024]{2,1,0:T(8,128)S(1)}, f32[3,32,1024]{2,1,0:T(8,128)}, u32[]{:S(2)}) copy-start(f32[3,32,1024]{2,1,0:T(8,128)} %get-tuple-element.25) | copy-start | bytes 1179652
  481.9 31.2 %copy-start.11 = (bf16[1,512,1024]{2,1,0:T(8,128)(2,1)S(1)}, bf16[1,512,1024]{2,1,0:T(8,128)(2,1)}, u32[]{:S(2)}) copy-start(bf16[1,512,1024]{2,1,0:T(8,128)(2,1)} %get-tuple-element.28) | copy-start | bytes 3145732
  481.9 31.2 %copy-start.12 = (bf16[1,512,1024]{2,1,0:T(8,128)(2,1)S(1)}, bf16[1,512,1024]{2,1,0:T(8,128)(2,1)}, u32[]{:S(2)}) copy-start(bf16[1,512,1024]{2,1,0:T(8,128)(2,1)} %get-tuple-element.29) | copy-start | bytes 3145732
where the time goes:
time: 595 us; the launch traced here: 588 us
  local copies, waits for them, and re-layouts  218 us (37%)
  blocking collectives  214 us (36%)
  other arithmetic  99.8 us (17%)
  matrix products  41 us (7%)
  starting transfers between devices  14.3 us (2%)
    psum x1, blocking collectives, on_device(): lax.psum((variance_local, intersection_local), 'freq')  155 us
    unnamed x42, local copies, waits for them, and re-layouts  114 us
    another operation x7, other arithmetic  66.4 us
    psum x1, blocking collectives, on_device(): spread = modulus * lax.psum(spread_local, 'freq')  51.9 us
    all_to_all x1, local copies, waits for them, and re-layouts, on_device(): lax.all_to_all(lag_one, 'freq', split_axis=3, concat_axis=2, tiled=True)  31.2 us
    another operation x1, local copies, waits for them, and re-layouts, on_device(): lag_one = jnp.stack([real_part, imag_part], axis=1).astype(jnp.bfloat16)  28.5 us
    reshape x1, local copies, waits for them, and re-layouts, on_device(): lag_grid = lags.reshape(template_count, DET, RESP, 2, N1, local_cols)  20.8 us
    dot_general x1, matrix products, on_device(): jnp.einsum('ipkm,pmq->ikq', filtered, complex_table(N2, 1.0), preferred_e...  18.9 us
  transfers between devices with their start and end apart: 2, of which 0 were waited for; matrix products, arithmetic and copies ran while one was open for 13% of the time, Pallas kernels for 0%

commit v1 on v0

--- a/solution.py
+++ b/solution.py
@@ -109,7 +109,12 @@
     table_row = complex_table(N1, 1.0)
     lags = jnp.einsum(
         "ipkc,pkq->iqc",
-        lax.all_to_all(lag_one, "freq", split_axis=3, concat_axis=2, tiled=True),
+        jnp.concatenate(
+            lax.all_to_all(
+                jnp.stack(jnp.split(lag_one, lax.axis_size("freq"), axis=3)), "freq", 0, 0
+            ),
+            axis=2,
+        ),
         table_row,
         preferred_element_type=jnp.float32,
     )

time: 595 us -> 499 us (0.84)
  local copies, waits for them, and re-layouts: 218 us -> 118 us
    unnamed x42, local copies, waits for them, and re-layouts: 114 us -> 56.4 us
    all_to_all x1 -> x0, local copies, waits for them, and re-layouts: 31.2 us -> none  [on_device(): lax.all_to_all(lag_one, 'freq', split_axis=3, concat_axis=2, tiled=True)]
    another operation x1 -> x0, local copies, waits for them, and re-layouts: 28.5 us -> none  [on_device(): lag_one = jnp.stack([real_part, imag_part], axis=1).astype(jnp.bfloat16)]
    reshape x0 -> x2, local copies, waits for them, and re-layouts: none -> 16.7 us  [on_device(): jnp.concatenate(lax.all_to_all(jnp.stack(jnp.split(lag_one, lax.axis_size...]
    unnamed x2 -> x17, other arithmetic: 3.38 us -> 9.89 us
    another operation x7 -> x8, other arithmetic: 66.4 us -> 67 us
  transfers between devices with their start and end apart: 2 -> 2, of which waited for: 0 -> 0; matrix products, arithmetic and copies ran while one was open for 13% -> 15% of each run, Pallas kernels for 0% -> 0%
where the time goes in v1:
time: 499 us; the launch traced here: 491 us
  blocking collectives  214 us (43%)
  local copies, waits for them, and re-layouts  118 us (24%)
  other arithmetic  103 us (21%)
  matrix products  42.6 us (9%)
  starting transfers between devices  14.1 us (3%)
    psum x1, blocking collectives, on_device(): lax.psum((variance_local, intersection_local), 'freq')  155 us
    another operation x7, other arithmetic  66.4 us
    unnamed x42, local copies, waits for them, and re-layouts  56.4 us
    psum x1, blocking collectives, on_device(): spread = modulus * lax.psum(spread_local, 'freq')  51.9 us
    reshape x1, local copies, waits for them, and re-layouts, on_device(): lag_grid = lags.reshape(template_count, DET, RESP, 2, N1, local_cols)  20.9 us
    dot_general x1, matrix products, on_device(): jnp.einsum('ipkm,pmq->ikq', filtered, complex_table(N2, 1.0), preferred_e...  20.3 us
    slice x1, local copies, waits for them, and re-layouts, on_device(): lag_grid[:, :, :, 0]  17.1 us
    reshape x2, local copies, waits for them, and re-layouts, on_device(): jnp.concatenate(lax.all_to_all(jnp.stack(jnp.split(lag_one, lax.axis_size...  16.7 us
  transfers between devices with their start and end apart: 2, of which 0 were waited for; matrix products, arithmetic and copies ran while one was open for 15% of the time, Pallas kernels for 0%

profile of v1, /device:TPU:0, one launch (start us, length us, event | category | flops | bytes accessed | tf_op | source)
XLA Modules:
  0.0 491.5 jit_solution(1415033704592700640)
XLA Ops:
  0.0 4.3 multiply_convert_fusion.3
  4.4 0.7 broadcast_add_fusion.1
  5.1 0.8 copy.85
  5.9 1.1 fusion.87
  7.4 1.3 convolution_bitcast_fusion.1
  8.7 0.7 reshape.225
  10.0 0.9 copy.110
  10.9 0.9 copy.111
  11.7 1.7 subtract_convert_fusion.1
  13.4 2.1 fusion.99
  15.5 1.3 reshape.237
  16.8 7.6 %all-to-all-start = ((bf16[16,2,6144]{2,1,0:T(2,128)(2,1)}), bf16[16,2,6144]{2,1,0:T(2,128)(2,1)}, u32[]{:S(2)}, u32[]{:S(2)}) async-start(bf16[16,2,6144]{2,1,0:T(2,128)(2,1)} %reshape.237), calls=%async_computation | async-start | bytes 786432 | tf_op jit(solution)/shard_map/all_to_all | solution.py:78
  24.5 16.6 %negate_convert_fusion = (bf16[1024,1024]{1,0:T(8,128)(2,1)S(1)}, bf16[1024,1024]{1,0:T(8,128)(2,1)}) fusion(), kind=kLoop, calls=%fused_computation.70 | loop fusion | flops 19922944 | bytes 4194304 | tf_op jit(solution)/shard_map/convert.7
  41.1 17.8 %cosine_convert_fusion = (bf16[1024,1024]{1,0:T(8,128)(2,1)}, bf16[1024,1024]{1,0:T(8,128)(2,1)}) fusion(), kind=kLoop, calls=%fused_computation.72 | loop fusion | flops 17825792 | bytes 4194304 | tf_op jit(solution)/shard_map/convert.22
  58.9 16.4 %fusion.32 = bf16[1024,1024]{1,0:T(8,128)(2,1)} fusion(), kind=kLoop, calls=%fused_computation.84 | loop fusion | flops 15728640 | bytes 2097152 | tf_op jit(solution)/shard_map/convert.11
  75.3 1.2 convert_bitcast_fusion.1
  77.1 1.5 concatenate.38
  78.6 9.4 %fusion.18 = (bf16[1,1024,2048]{2,1,0:T(8,128)(2,1)}, bf16[1,1024,2048]{2,1,0:T(8,128)(2,1)}, bf16[1,1024,2048]{2,1,0:T(8,128)(2,1)}, bf16[1,1024,2048]{2,1,0:T(8,128)(2,1)}) fusion(bf16[1024,1024]{1,0:T(8,128)(2,1)} %get-tuple-element.38, bf16[1024,1024]{1,0:T(8,128)(2,1)} %get-tuple-element.39, bf16[1024,1024]{1,0:T(8,128)(2,1)S(1)} %get-tuple-element.36, ...), kind=kLoop, calls=%fused_computation.65 | loop fusion | flops 29360128 | bytes 27262976 | tf_op jit(solution)/shard_map/stack | solution.py:30
  88.1 2.5 reshape.238
  91.6 4.4 fusion.28
  96.0 0.9 slice_multiply_fusion.1
  97.7 5.6 %multiply_convert_fusion.1 = (bf16[4,3,5,32,1024]{4,3,2,1,0:T(8,128)(2,1)}, bf16[4,3,5,32,1024]{4,3,2,1,0:T(8,128)(2,1)}) fusion(f32[3,5,32,1024]{3,2,1,0:T(8,128)S(1)} %copy-done.2, f32[4,3,32,1024]{3,2,1,0:T(8,128)S(1)} %get-tuple-element.19, f32[4,3,32,1024]{3,2,1,0:T(8,128)S(1)} %get-tuple-element.20), kind=kLoop, calls=%fused_computation.46 | loop fusion | flops 7864320 | bytes 12976128 | tf_op jit(solution)/shard_map/convert.15
  103.3 20.3 %fusion.13 = f32[60,32,2048]{2,1,0:T(8,128)S(1)} fusion(bf16[1,1024,2048]{2,1,0:T(8,128)(2,1)S(1)} %copy-done.3, bf16[1,1024,2048]{2,1,0:T(8,128)(2,1)} %get-tuple-element.13, bf16[60,1,32,1024]{3,2,1,0:T(8,128)(2,1)} %bitcast.140, bf16[60,1,32,1024]{3,2,1,0:T(8,128)(2,1)} %bitcast.139), kind=kOutput, calls=%fused_computation.58 | convolution fusion | flops 16114253824 | bytes 31981568 | tf_op jit(solution)/shard_map/ipkm,pmq->ikq/dot_general | solution.py:102
  123.6 2.8 fusion.26
  133.6 5.5 %copy-done = bf16[16,60,2,32,64]{4,3,1,2,0:T(8,128)(2,1)} copy-done((bf16[16,60,2,32,64]{4,3,1,2,0:T(8,128)(2,1)}, bf16[16,60,2,32,64]{4,3,1,2,0:T(8,128)(2,1)S(1)}, u32[]{:S(2)}) %copy-start) | copy-done | bytes 7864344
  139.1 18.7 %reshape.239 = bf16[16,2,122880]{2,1,0:T(2,128)(2,1)} reshape(bf16[16,2,60,32,64]{4,3,2,1,0:T(8,128)(2,1)} %bitcast.137) | data formatting | bytes 15728640
  157.9 6.5 %all-to-all-start.1 = ((bf16[16,2,122880]{2,1,0:T(2,128)(2,1)}), bf16[16,2,122880]{2,1,0:T(2,128)(2,1)}, u32[]{:S(2)}, u32[]{:S(2)}) async-start(bf16[16,2,122880]{2,1,0:T(2,128)(2,1)} %reshape.239), calls=%async_computation.1 | async-start | bytes 15728640 | tf_op jit(solution)/shard_map/all_to_all | solution.py:113
  165.0 4.0 negate_convert_fusion.2
  169.0 1.6 fusion.38
  170.7 1.5 fusion.35
  172.2 0.8 broadcast_multiply_fusion
  173.0 154.6 %all-reduce.1 = (f32[4,3,4]{2,0,1:T(4,128)S(1)}, f32[4,3]{0,1:T(4,128)S(1)}) all-reduce(f32[4,3,4]{2,0,1:T(4,128)S(1)} %fusion.35, f32[4,3]{0,1:T(4,128)S(1)} %get-tuple-element.24), channel_id=1, replica_groups=mesh['tmpl'=2,'freq'=16] {'freq'}, use_global_device_ids=true, to_apply=%region_3.4 | all-reduce | flops 60 | bytes 480 | tf_op jit(solution)/shard_map/psum | solution.py:126
  327.8 0.9 copy.99
  328.8 1.0 fusion.7
  329.8 51.9 %psum.23 = f32[4,3,4]{2,0,1:T(4,128)S(1)} all-reduce(f32[4,3,4]{2,0,1:T(4,128)S(1)} %copy.101), channel_id=1, replica_groups=mesh['tmpl'=2,'freq'=16] {'freq'}, use_global_device_ids=true, to_apply=%region_5.6 | all-reduce | flops 48 | bytes 384 | tf_op jit(solution)/shard_map/psum | solution.py:130
  382.0 18.5 %reshape.240 = bf16[16,2,60,32,64]{4,3,2,1,0:T(8,128)(2,1)} reshape(bf16[16,2,122880]{2,1,0:T(2,128)(2,1)} %all-to-all-done.1) | data formatting | bytes 15728640
  400.5 8.7 %bitcast_bitcast_fusion = bf16[60,2,16,32,64]{4,3,0,1,2:T(8,128)(2,1)S(1)} fusion(bf16[16,2,60,32,64]{4,3,2,1,0:T(8,128)(2,1)} %reshape.240), kind=kLoop, calls=%fused_computation.207 | loop fusion | bytes 15728640 | tf_op jit(solution)/shard_map/reshape | solution.py:112
  409.2 8.0 %copy.91 = bf16[60,2,16,32,64]{4,3,2,1,0:T(8,128)(2,1)} copy(bf16[60,2,16,32,64]{4,3,0,1,2:T(8,128)(2,1)S(1)} %bitcast_bitcast_fusion) | data formatting | bytes 15728640 | tf_op jit(solution)/shard_map/reshape | solution.py:112
  417.2 15.1 %convolution_bitcast_fusion = f32[60,1024,64]{1,2,0:T(8,128)} fusion(bf16[60,2,512,64]{3,2,1,0:T(8,128)(2,1)} %bitcast.138, bf16[1,512,1024]{2,1,0:T(8,128)(2,1)S(1)} %copy-done.13, bf16[1,512,1024]{2,1,0:T(8,128)(2,1)S(1)} %copy-done.12), kind=kOutput, calls=%fused_computation.31 | convolution fusion | flops 8057257984 | bytes 25690112 | tf_op jit(solution)/shard_map/ipkc,pkq->iqc/dot_general | solution.py:110
  432.3 20.9 %reshape.228 = f32[4,3,5,2,512,64]{4,3,5,2,1,0:T(2,128)} reshape(f32[60,1024,64]{1,2,0:T(8,128)} %convolution_bitcast_fusion) | data formatting | bytes 31457280 | tf_op jit(solution)/shard_map/reshape | solution.py:132
  453.2 17.1 %fusion.97 = (f32[4,3,5,1,512,64]{4,3,5,2,1,0:T(1,128)S(1)}, f32[4,3,5,1,512,64]{4,3,5,2,1,0:T(1,128)}) fusion(f32[4,3,5,2,512,64]{4,3,5,2,1,0:T(2,128)} %reshape.228), kind=kLoop, calls=%fused_computation.205 | loop fusion | bytes 31457280 | tf_op jit(solution)/shard_map/slice | solution.py:133
  470.3 4.3 copy.118
  474.7 1.6 copy.119
  476.5 2.7 fusion.12
  480.6 1.3 reduce.2
  482.1 7.1 %all_to_all.35 = f32[2,1,16384]{2,1,0:T(1,128)S(1)} all-to-all(f32[2,1,16384]{2,1,0:T(1,128)S(1)} %reshape.241), channel_id=1, replica_groups=mesh['tmpl'=2,'freq'=16] {'tmpl'}, dimensions={0} | all-to-all | bytes 262144 | tf_op jit(solution)/shard_map/all_to_all | solution.py:135
  489.1 1.0 reduce.3
  490.5 0.7 copy.104
  (79 shorter events, 13.7 us)
Async XLA Ops:
  4.4 3.0 copy-start.9
  16.8 71.2 %all-to-all-start = ((bf16[16,2,6144]{2,1,0:T(2,128)(2,1)}), bf16[16,2,6144]{2,1,0:T(2,128)(2,1)}, u32[]{:S(2)}, u32[]{:S(2)}) async-start(bf16[16,2,6144]{2,1,0:T(2,128)(2,1)} %reshape.237), calls=%async_computation | async-start | bytes 786432 | tf_op jit(solution)/shard_map/all_to_all | solution.py:78
  24.5 50.8 %copy-start.7 = (bf16[4,2,32,1024]{3,2,1,0:T(8,128)(2,1)S(1)}, bf16[4,2,32,1024]{3,2,1,0:T(8,128)(2,1)}, u32[]{:S(2)}) copy-start(bf16[4,2,32,1024]{3,2,1,0:T(8,128)(2,1)} %param.8) | copy-start | bytes 1572868
  41.1 36.0 %copy-start.4 = (bf16[3,4,32,1024]{3,2,1,0:T(8,128)(2,1)S(1)}, bf16[3,4,32,1024]{3,2,1,0:T(8,128)(2,1)}, u32[]{:S(2)}) copy-start(bf16[3,4,32,1024]{3,2,1,0:T(8,128)(2,1)} %param.9) | copy-start | bytes 2359300
  76.5 2.2 copy-start.1
  91.6 4.4 copy-start.14
  91.6 5.3 %copy-start.5 = (f32[4,32,1024]{2,1,0:T(8,128)S(1)}, f32[4,32,1024]{2,1,0:T(8,128)}, u32[]{:S(2)}) copy-start(f32[4,32,1024]{2,1,0:T(8,128)} %get-tuple-element.30) | copy-start | bytes 1572868
  91.6 5.3 %copy-start.6 = (f32[4,32,1024]{2,1,0:T(8,128)S(1)}, f32[4,32,1024]{2,1,0:T(8,128)}, u32[]{:S(2)}) copy-start(f32[4,32,1024]{2,1,0:T(8,128)} %get-tuple-element.31) | copy-start | bytes 1572868
  96.0 1.7 copy-start.2
  97.7 5.6 %copy-start.3 = (bf16[1,1024,2048]{2,1,0:T(8,128)(2,1)S(1)}, bf16[1,1024,2048]{2,1,0:T(8,128)(2,1)}, u32[]{:S(2)}) copy-start(bf16[1,1024,2048]{2,1,0:T(8,128)(2,1)} %get-tuple-element.12) | copy-start | bytes 12582916
  133.6 5.5 %copy-start = (bf16[16,60,2,32,64]{4,3,1,2,0:T(8,128)(2,1)}, bf16[16,60,2,32,64]{4,3,1,2,0:T(8,128)(2,1)S(1)}, u32[]{:S(2)}) copy-start(bf16[16,60,2,32,64]{4,3,1,2,0:T(8,128)(2,1)S(1)} %fusion.64) | copy-start | bytes 23592964
  157.9 6.7 %copy-start.8 = (bf16[4,2,32,1024]{3,2,1,0:T(8,128)(2,1)S(1)}, bf16[4,2,32,1024]{3,2,1,0:T(8,128)(2,1)}, u32[]{:S(2)}) copy-start(bf16[4,2,32,1024]{3,2,1,0:T(8,128)(2,1)} %param.8) | copy-start | bytes 1572868
  157.9 224.1 %all-to-all-start.1 = ((bf16[16,2,122880]{2,1,0:T(2,128)(2,1)}), bf16[16,2,122880]{2,1,0:T(2,128)(2,1)}, u32[]{:S(2)}, u32[]{:S(2)}) async-start(bf16[16,2,122880]{2,1,0:T(2,128)(2,1)} %reshape.239), calls=%async_computation.1 | async-start | bytes 15728640 | tf_op jit(solution)/shard_map/all_to_all | solution.py:113
  164.3 4.7 copy-start.10
  164.3 6.3 %copy-start.11 = (f32[3,32,1024]{2,1,0:T(8,128)S(1)}, f32[3,32,1024]{2,1,0:T(8,128)}, u32[]{:S(2)}) copy-start(f32[3,32,1024]{2,1,0:T(8,128)} %get-tuple-element.25) | copy-start | bytes 1179652
  409.2 8.0 %copy-start.12 = (bf16[1,512,1024]{2,1,0:T(8,128)(2,1)S(1)}, bf16[1,512,1024]{2,1,0:T(8,128)(2,1)}, u32[]{:S(2)}) copy-start(bf16[1,512,1024]{2,1,0:T(8,128)(2,1)} %get-tuple-element.28) | copy-start | bytes 3145732
  409.2 8.0 %copy-start.13 = (bf16[1,512,1024]{2,1,0:T(8,128)(2,1)S(1)}, bf16[1,512,1024]{2,1,0:T(8,128)(2,1)}, u32[]{:S(2)}) copy-start(bf16[1,512,1024]{2,1,0:T(8,128)(2,1)} %get-tuple-element.29) | copy-start | bytes 3145732
